TPU v7x, 128 devices: a whole 4x4x4 slice. The times are simulated.
128 devices in a mesh: orb: 8 (over x, y_lo), aux: 16 (over z, y_hi, core).
Axes of the slice: x: 4, y: 4 (y_hi: 2, y_lo: 2; y = y_hi * 2 + y_lo), z: 4, core: 2. Of those that a mesh axis runs over, the one named last changes fastest.
Arguments:
- raw_rows: bfloat16 [512, 2048, 128], P('orb', 'aux'), may hold values from -4 to 4
- fit_metric: bfloat16 [512, 512, 512], P(('orb', 'aux'))
- domain: int32 [512, 512], P('orb'), may hold values from 0 to 127, as said below
- counts: int32 [512, 16], P('orb'), may hold values from 16 to 64, as said below
- orbital_ids: int32 [512], P(('orb', 'aux')), may hold values from 0 to 511, each once
- occ_energy: float32 [512], replicated, may hold values from -1.5 to -0.3
- osv_energy: bfloat16 [512, 128], P(('orb', 'aux')), may hold values from 0.29882812 to 3
- matchings: int32 [4, 8], replicated, may hold values from 0 to 7, as said below
- screening: int32 [512, 5, 4], P(('orb', 'aux')), may hold values 0 or 1
Outputs:
- density: float32 [512, 2048, 128], P('orb', 'aux')
- pair_energy: float32 [512, 5, 4], P(('orb', 'aux'))
Inputs may be any that keep to these rules, and one draw needn't show every extreme that they name: `counts`: every row sums to 512; every entry is at most 64, and every row has an entry equal to 64. `domain`: the positions of a row are taken by owner 0 first, then owner 1 and so on, in the numbers that counts gives; within one owner's run the entries are distinct. `matchings`: row q maps orb index o to o XOR m_q, with a mask m_q from 1 to 7; rounds may repeat a mask.
All inputs are finite; a program needn't handle non-finite values. No bound on the sum of `screening` on one device may be relied on, other than what follows from the above.
Results may differ from a plain program's by a relative error of at most 0.0029.
Values may be sent and summed in bfloat16 or wider, within the bound.
No kernel may reach another device: no remote copies, remote signals or barrier semaphores. Data moves between devices by JAX's collectives and lax.ppermute only.
A program may use at most 128 MiB of HBM per device.

v0:
```python
import jax
import jax.numpy as jnp
from jax import lax
from jax.sharding import PartitionSpec as P

PAIR_SCALE = 1.3


def as_sent(x):

    def short(part):
        return part.astype(jnp.bfloat16) if part.dtype == jnp.float32 else part

    return jax.tree.map(short, x)


def partner(x, axis, stride):
    return lax.ppermute(x, axis, [(i, i ^ 1 << stride) for i in range(lax.axis_size(axis))])


def lookup_energy(identities, energy_table):
    everyone = jnp.arange(energy_table.shape[0], dtype=jnp.int32)
    return jnp.sum(
        jnp.where(identities[:, None] == everyone[None, :], energy_table[None, :], 0.0), axis=1
    )


def pair_terms(density, raw_full, own_occ, own_osv, partner_block, occ_energy, screen_round):
    far_fitted, far_rows, far_osv, far_names = partner_block
    orbitals, aux_total, osv_count = raw_full.shape
    far_occ = lookup_energy(far_names, occ_energy)
    spread_out = jnp.zeros((orbitals, aux_total, osv_count), jnp.bfloat16)
    spread_out = spread_out.at[jnp.arange(orbitals, dtype=jnp.int32)[:, None], far_rows].set(
        far_fitted
    )
    integrals = jnp.einsum(
        "kpa,lpb->klab", raw_full, spread_out, preferred_element_type=jnp.float32
    )
    denominator = (
        own_osv[:, None, :, None]
        + far_osv.astype(jnp.float32)[None, :, None, :]
        - own_occ[:, None, None, None]
        - far_occ[None, :, None, None]
    )
    amplitudes = (screen_round[:, :, None, None] * integrals / denominator).astype(jnp.bfloat16)
    widened = lax.optimization_barrier(amplitudes).astype(jnp.float32)
    energy = PAIR_SCALE * jnp.sum(widened * integrals, axis=(2, 3)) / (osv_count * osv_count)
    density = density + jnp.einsum(
        "klab,lpb->kpa", amplitudes, spread_out, preferred_element_type=jnp.float32
    )
    return (density, energy)


def per_device(
    raw_rows, fit_metric, domain, counts, orbital_ids, occ_energy, osv_energy, matchings, screening
):
    aux_count = lax.axis_size("aux")
    my_aux = lax.axis_index("aux")
    group_slots, aux_dev, osv_count = raw_rows.shape
    fit_count = domain.shape[1]
    orbitals = group_slots // aux_count
    capacity = 2 * fit_count // aux_count
    aux_total = aux_dev * aux_count
    run_ends = jnp.cumsum(counts, axis=1)
    run_starts = run_ends - counts
    slot_index = jnp.arange(capacity, dtype=jnp.int32)
    send_start = lax.dynamic_index_in_dim(run_starts, my_aux, 1, keepdims=False)
    send_count = lax.dynamic_index_in_dim(counts, my_aux, 1, keepdims=False)
    is_valid = slot_index[None, :] < send_count[:, None]
    where_at = jnp.minimum(send_start[:, None] + slot_index[None, :], fit_count - 1)
    local_rows = jnp.where(is_valid, jnp.take_along_axis(domain, where_at, axis=1), 0)
    flat_index = jnp.arange(group_slots, dtype=jnp.int32)[:, None] * aux_dev + local_rows
    packed = jnp.take(raw_rows.reshape(group_slots * aux_dev, osv_count), flat_index, axis=0)
    packed = jnp.where(is_valid[:, :, None], packed, jnp.zeros((), jnp.bfloat16))
    packed = packed.reshape(aux_count, orbitals, capacity, osv_count)
    received = lax.all_to_all(packed, "aux", split_axis=0, concat_axis=0, tiled=True)
    own_counts = lax.dynamic_slice_in_dim(counts, my_aux * orbitals, orbitals, 0)
    own_domain = lax.dynamic_slice_in_dim(domain, my_aux * orbitals, orbitals, 0)
    own_ends = jnp.cumsum(own_counts, axis=1)
    own_starts = own_ends - own_counts
    positions = jnp.arange(fit_count, dtype=jnp.int32)
    source = jnp.sum((positions[None, :, None] >= own_ends[:, None, :]).astype(jnp.int32), axis=2)
    offset = positions[None, :] - jnp.take_along_axis(own_starts, source, axis=1)
    local_range = jnp.arange(orbitals, dtype=jnp.int32)
    gather_index = (source * orbitals + local_range[:, None]) * capacity + offset
    gathered_rows = jnp.take(
        received.reshape(aux_count * orbitals * capacity, osv_count), gather_index, axis=0
    )
    rows_global = source * aux_dev + own_domain
    fitted = jnp.einsum(
        "kpq,kqa->kpa", fit_metric, gathered_rows, preferred_element_type=jnp.float32
    ).astype(jnp.bfloat16)
    raw_full = jnp.zeros((orbitals, aux_total, osv_count), jnp.bfloat16)
    raw_full = raw_full.at[local_range[:, None], rows_global].set(gathered_rows)
    own_occ = lookup_energy(orbital_ids, occ_energy)
    own_osv = osv_energy.astype(jnp.float32)
    screen_all = screening.astype(jnp.float32)
    own_block = (fitted, rows_global, osv_energy, orbital_ids)
    density = jnp.zeros((orbitals, aux_total, osv_count), jnp.float32)
    density, energy = pair_terms(
        density, raw_full, own_occ, own_osv, own_block, occ_energy, screen_all[:, 0]
    )
    energies = [energy]
    matches = matchings.shape[0]
    orb_count = lax.axis_size("orb")
    bit_total = orb_count.bit_length() - 1
    for round_index in range(matches):
        round_mask = matchings[round_index, 0]
        partner_block = own_block
        for bit_number in range(bit_total):
            swapped = jax.tree.map(
                lambda part, own: part.astype(own.dtype),
                partner(as_sent(partner_block), "orb", bit_number),
                partner_block,
            )
            take_swap = round_mask >> bit_number & 1 == 1
            partner_block = tuple(
                (
                    jnp.where(take_swap, arrived, unchanged)
                    for arrived, unchanged in zip(swapped, partner_block)
                )
            )
        density, energy = pair_terms(
            density,
            raw_full,
            own_occ,
            own_osv,
            partner_block,
            occ_energy,
            screen_all[:, round_index + 1],
        )
        energies.append(energy)
    returned = lax.all_to_all(density, "aux", split_axis=1, concat_axis=0, tiled=True)
    return (returned, jnp.stack(energies, axis=1))


def solution(mesh):
    placed = (
        P("orb", "aux", None),
        P(("orb", "aux"), None, None),
        P("orb", None),
        P("orb", None),
        P(("orb", "aux")),
        P(),
        P(("orb", "aux"), None),
        P(),
        P(("orb", "aux"), None, None),
    )
    return jax.shard_map(
        per_device,
        mesh=mesh,
        in_specs=placed,
        out_specs=(P("orb", "aux", None), P(("orb", "aux"), None, None)),
        check_vma=False,
    )
```

profile of v0, /device:TPU:1, one launch (start us, length us, event | category | flops | bytes accessed | tf_op | source)
XLA Modules:
  0.0 398.5 jit_solution(3829162994728119619)
XLA Ops:
  0.7 2.2 collective-permute-start.9
  7.5 32.8 %gather_fusion.3 = s32[4096]{0:T(1024)S(1)} fusion(s32[64,512]{1,0:T(8,128)S(1)} %copy-done.2, s32[4096]{0:T(1024)S(1)} %reshape.547), kind=kCustom, calls=%fused_computation.3 | custom fusion | bytes 65536 | tf_op jit(solution)/shard_map/jit(take_along_axis)/gather | solution.py:71
  40.7 12.1 %gather_fusion = bf16[4096,128]{1,0:T(8,128)(2,1)S(1)} fusion(bf16[8192,128]{1,0:T(8,128)(2,1)S(1)} %bitcast.213, s32[4096]{0:T(1024)S(1)} %broadcast_clamp_fusion), kind=kCustom, calls=%fused_computation | custom fusion | bytes 2113536 | tf_op jit(solution)/shard_map/jit(_take)/gather | solution.py:73
  53.0 2.5 select_select_fusion
  55.4 9.2 %all-to-all-start = ((bf16[16,4,64,128]{3,2,1,0:T(8,128)(2,1)}), bf16[16,4,64,128]{3,2,1,0:T(8,128)(2,1)S(1)}, u32[]{:S(2)}, u32[]{:S(2)}) async-start(bf16[16,4,64,128]{3,2,1,0:T(8,128)(2,1)} %select_select_fusion), calls=%async_computation | async-start | bytes 2097152 | tf_op jit(solution)/shard_map/all_to_all | solution.py:76
  72.9 17.6 %gather_fusion.2 = s32[2048]{0:T(1024)S(1)} fusion(s32[4,16]{1,0:T(4,128)S(1)} %fusion.57, s32[2048]{0:T(1024)S(1)} %bitcast.214), kind=kCustom, calls=%fused_computation.2 | custom fusion | bytes 32768 | tf_op jit(solution)/shard_map/jit(take_along_axis)/gather | solution.py:83
  95.0 2.5 collective-permute-start.27
  98.0 2.4 collective-permute-start.19
  101.9 2.4 collective-permute-done.11
  108.7 2.1 collective-permute-start.25
  111.9 2.1 collective-permute-start.8
  118.0 2.5 collective-permute-start.21
  121.1 2.5 collective-permute-start.13
  125.2 2.5 collective-permute-done.2
  127.8 6.2 %gather_fusion.1 = bf16[2048,128]{1,0:T(8,128)(2,1)S(1)} fusion(bf16[4096,128]{1,0:T(8,128)(2,1)S(1)} %bitcast.222, s32[2048]{0:T(1024)S(1)} %broadcast_clamp_fusion.1), kind=kCustom, calls=%fused_computation.1 | custom fusion | bytes 1056768 | tf_op jit(solution)/shard_map/jit(_take)/gather | solution.py:86
  134.3 2.4 fusion.1
  137.3 7.9 %collective-permute-done.3 = bf16[4,512,128]{1,2,0:T(8,128)(2,1)S(1)} collective-permute-done((bf16[4,512,128]{1,2,0:T(8,128)(2,1)S(1)}, bf16[4,512,128]{1,2,0:T(8,128)(2,1)S(1)}, u32[]{:S(2)}, u32[]{:S(2)}) %collective-permute-start.3) | collective-permute-done | bytes 524320 | tf_op jit(solution)/shard_map/ppermute | solution.py:18
  146.9 7.4 %scatter_custom_fusion = bf16[8192,128]{1,0:T(8,128)(2,1)} fusion(s32[2048]{0:T(1024)S(1)} %bitcast.245, bf16[2048,128]{1,0:T(8,128)(2,1)S(1)} %bitcast.239, bf16[]{:T(256)} %constant.130.clone.1), kind=kCustom, calls=%fused_computation.32 | custom fusion | bytes 2097154
  154.3 6.5 %scatter_custom_fusion.1 = bf16[8192,128]{1,0:T(8,128)(2,1)S(1)} fusion(s32[2048]{0:T(1024)S(1)} %bitcast.246, bf16[2048,128]{1,0:T(8,128)(2,1)S(1)} %bitcast.234, bf16[]{:T(256)} %constant.130.clone.1), kind=kCustom, calls=%fused_computation.30 | custom fusion | bytes 2097154
  162.4 2.9 convolution_bitcast_fusion.4
  168.8 2.4 collective-permute-done.22
  174.0 4.9 %collective-permute-done.14 = bf16[4,512,128]{1,2,0:T(8,128)(2,1)S(1)} collective-permute-done((bf16[4,512,128]{1,2,0:T(8,128)(2,1)S(1)}, bf16[4,512,128]{1,2,0:T(8,128)(2,1)S(1)}, u32[]{:S(2)}, u32[]{:S(2)}) %collective-permute-start.14) | collective-permute-done | bytes 524320 | tf_op jit(solution)/shard_map/ppermute | solution.py:18
  180.9 9.2 %collective-permute-done.4 = bf16[4,512,128]{1,2,0:T(8,128)(2,1)S(1)} collective-permute-done((bf16[4,512,128]{1,2,0:T(8,128)(2,1)S(1)}, bf16[4,512,128]{1,2,0:T(8,128)(2,1)S(1)}, u32[]{:S(2)}, u32[]{:S(2)}) %collective-permute-start.4) | collective-permute-done | bytes 524320 | tf_op jit(solution)/shard_map/ppermute | solution.py:18
  192.2 10.8 %collective-permute-done.31 = bf16[4,512,128]{1,2,0:T(8,128)(2,1)S(1)} collective-permute-done((bf16[4,512,128]{1,2,0:T(8,128)(2,1)S(1)}, bf16[4,512,128]{1,2,0:T(8,128)(2,1)S(1)}, u32[]{:S(2)}, u32[]{:S(2)}) %collective-permute-start.31) | collective-permute-done | bytes 524320 | tf_op jit(solution)/shard_map/ppermute | solution.py:18
  203.9 2.1 copy.110
  205.9 8.6 %collective-permute-done.23 = bf16[4,512,128]{1,2,0:T(8,128)(2,1)} collective-permute-done((bf16[4,512,128]{1,2,0:T(8,128)(2,1)}, bf16[4,512,128]{1,2,0:T(8,128)(2,1)}, u32[]{:S(2)}, u32[]{:S(2)}) %collective-permute-start.23) | collective-permute-done | bytes 524320 | tf_op jit(solution)/shard_map/ppermute | solution.py:18
  216.4 2.0 copy.106
  218.5 7.4 %collective-permute-done.15 = bf16[4,512,128]{1,2,0:T(8,128)(2,1)} collective-permute-done((bf16[4,512,128]{1,2,0:T(8,128)(2,1)}, bf16[4,512,128]{1,2,0:T(8,128)(2,1)}, u32[]{:S(2)}, u32[]{:S(2)}) %collective-permute-start.15) | collective-permute-done | bytes 524320 | tf_op jit(solution)/shard_map/ppermute | solution.py:18
  227.8 2.1 copy.102
  229.8 7.3 %collective-permute-done.5 = bf16[4,512,128]{1,2,0:T(8,128)(2,1)} collective-permute-done((bf16[4,512,128]{1,2,0:T(8,128)(2,1)}, bf16[4,512,128]{1,2,0:T(8,128)(2,1)}, u32[]{:S(2)}, u32[]{:S(2)}) %collective-permute-start.5) | collective-permute-done | bytes 524320 | tf_op jit(solution)/shard_map/ppermute | solution.py:18
  237.1 1.9 broadcast_select_fusion.11
  239.0 2.0 copy.98
  241.0 17.2 %scatter_custom_fusion.4 = bf16[8192,128]{1,0:T(8,128)(2,1)} fusion(s32[2048]{0:T(1024)S(1)} %bitcast.244, bf16[2048,128]{1,0:T(8,128)(2,1)} %bitcast.237, bf16[]{:T(256)} %constant.130.clone.1), kind=kCustom, calls=%fused_computation.24 | custom fusion | bytes 2097664
  258.3 3.9 convolution_bitcast_fusion.1
  262.2 7.7 %scatter_custom_fusion.3 = bf16[8192,128]{1,0:T(8,128)(2,1)} fusion(s32[2048]{0:T(1024)S(1)} %bitcast.243, bf16[2048,128]{1,0:T(8,128)(2,1)} %bitcast.238, bf16[]{:T(256)} %constant.130.clone.1), kind=kCustom, calls=%fused_computation.26 | custom fusion | bytes 2097664
  269.9 3.8 convolution_bitcast_fusion.2
  273.8 7.8 %scatter_custom_fusion.5 = bf16[8192,128]{1,0:T(8,128)(2,1)} fusion(s32[2048]{0:T(1024)S(1)} %bitcast.241, bf16[2048,128]{1,0:T(8,128)(2,1)} %bitcast.235, bf16[]{:T(256)} %constant.130.clone.1), kind=kCustom, calls=%fused_computation.22 | custom fusion | bytes 2097664
  281.6 5.2 %divide_convert_fusion = (bf16[4,4,128,128]{2,3,0,1:T(8,128)(2,1)}, bf16[4,4,128,128]{2,3,0,1:T(8,128)(2,1)S(1)}, bf16[4,4,128,128]{2,3,0,1:T(8,128)(2,1)S(1)}, ...) fusion(f32[4]{0:T(128)S(1)} %get-tuple-element.20, f32[4,128]{1,0:T(4,128)S(1)} %select_convert_fusion, ...), kind=kOutput, calls=%fused_computation.39 | convolution fusion | flops 1080033280 | bytes 10494272 | tf_op jit(solution)/shard_map/kpa,lpb->klab/dot_general | solution.py:36
  286.7 3.2 fusion.33
  290.0 3.3 fusion.34
  293.3 3.2 fusion.31
  296.5 7.9 %scatter_custom_fusion.2 = bf16[8192,128]{1,0:T(8,128)(2,1)} fusion(s32[2048]{0:T(1024)S(1)} %bitcast.242, bf16[2048,128]{1,0:T(8,128)(2,1)} %bitcast.236, bf16[]{:T(256)} %constant.130.clone.1), kind=kCustom, calls=%fused_computation.28 | custom fusion | bytes 2097664
  304.4 4.0 %divide_convert_fusion.3 = (bf16[4,4,128,128]{2,3,0,1:T(8,128)(2,1)S(1)}, f32[4,4,128,128]{2,3,0,1:T(8,128)}) fusion(f32[4]{0:T(128)S(1)} %get-tuple-element.21, f32[4,128]{1,0:T(4,128)S(1)} %select_convert_fusion.3, f32[4,4]{0,1:T(4,128)S(1)} %bitcast.247, f32[4]{0:T(128)S(1)} %get-tuple-element.24, f32[4,128]{1,0:T(4,128)S(1)} %get-tuple-element.56, ...), kind=kOutput, calls=%fused_computation.42 | convolution fusion | flops 1075314688 | bytes 5771360 | tf_op jit(solution)/shard_map/kpa,lpb->klab/dot_general | solution.py:36
  314.0 2.0 fusion
  316.0 10.0 %copy.114 = f32[4,2048,128]{2,0,1:T(4,128)} copy(f32[4,2048,128]{2,1,0:T(8,128)S(1)} %fusion) | data formatting | bytes 8388608 | tf_op jit(solution)/shard_map/add | solution.py:48
  326.0 16.3 %all-to-all-start.1 = ((f32[4,2048,128]{2,0,1:T(4,128)}), f32[4,2048,128]{2,0,1:T(4,128)}, u32[]{:S(2)}, u32[]{:S(2)}) async-start(f32[4,2048,128]{2,0,1:T(4,128)} %copy.114), calls=%async_computation.1 | async-start | bytes 8388608 | tf_op jit(solution)/shard_map/all_to_all | solution.py:133
  350.6 42.8 %all-to-all-done.1 = f32[4,2048,128]{2,0,1:T(4,128)} async-done(((f32[4,2048,128]{2,0,1:T(4,128)}), f32[4,2048,128]{2,0,1:T(4,128)}, u32[]{:S(2)}, u32[]{:S(2)}) %all-to-all-start.1) | async-done | bytes 4194336 | tf_op jit(solution)/shard_map/all_to_all | solution.py:133
  393.3 5.0 %copy.115 = f32[16,4,128,128]{3,2,1,0:T(8,128)} copy(f32[16,4,128,128]{3,1,2,0:T(4,128)} %bitcast.70) | data formatting | bytes 8388608 | tf_op jit(solution)/shard_map/all_to_all | solution.py:133
  (218 shorter events, 56.7 us)
Async XLA Ops:
  0.6 40.1 %copy-start = (bf16[64,128,128]{2,1,0:T(8,128)(2,1)S(1)}, bf16[64,128,128]{2,1,0:T(8,128)(2,1)}, u32[]{:S(2)}) copy-start(bf16[64,128,128]{2,1,0:T(8,128)(2,1)} %param.9) | copy-start | bytes 6291460
  0.6 6.9 %copy-start.2 = (s32[64,512]{1,0:T(8,128)S(1)}, s32[64,512]{1,0:T(8,128)}, u32[]{:S(2)}) copy-start(s32[64,512]{1,0:T(8,128)} %param.11) | copy-start | bytes 393220
  0.7 90.6 %collective-permute-start.9 = (s32[4]{0:T(128)}, s32[4]{0:T(128)S(1)}, u32[]{:S(2)}, u32[]{:S(2)}) collective-permute-start(s32[4]{0:T(128)} %param.13), channel_id=1, source_target_pairs={{0,16},{16,0},{32,48},{48,32},{64,80},{80,64},{96,112},{112,96},{1... | collective-permute-start | bytes 56 | tf_op jit(solution)/shard_map/ppermute | solution.py:18
  2.9 101.5 %collective-permute-start.6 = (bf16[4,128]{1,0:T(4,128)(2,1)}, bf16[4,128]{1,0:T(4,128)(2,1)S(1)}, u32[]{:S(2)}, u32[]{:S(2)}) collective-permute-start(bf16[4,128]{1,0:T(4,128)(2,1)} %param.15), channel_id=1, source_target_pairs={{0,16},{16,0},{32,48},{48,32},{64,80},{80,64},{96,112},{112,96},{1... | collective-permute-start | bytes 3080 | tf_op jit(solution)/shard_map/ppermute | solution.py:18
  4.8 110.1 %collective-permute-start = (s32[4,512]{1,0:T(4,128)S(1)}, s32[4,512]{1,0:T(4,128)S(1)}, u32[]{:S(2)}, u32[]{:S(2)}) collective-permute-start(s32[4,512]{1,0:T(4,128)S(1)} %get-tuple-element.26), channel_id=1, source_target_pairs={{0,16},{16,0},{32,48},{48,32},{64,80},{80,64},{96,112},{112,96},{1... | collective-permute-start | bytes 24584 | tf_op jit(solution)/shard_map/ppermute | solution.py:18
  53.0 11.6 %copy-start.23 = (s32[4,8]{1,0:T(4,128)S(1)}, s32[4,8]{1,0:T(4,128)}, u32[]{:S(2)}) copy-start(s32[4,8]{1,0:T(4,128)} %param.16) | copy-start | bytes 388
  55.4 72.4 %all-to-all-start = ((bf16[16,4,64,128]{3,2,1,0:T(8,128)(2,1)}), bf16[16,4,64,128]{3,2,1,0:T(8,128)(2,1)S(1)}, u32[]{:S(2)}, u32[]{:S(2)}) async-start(bf16[16,4,64,128]{3,2,1,0:T(8,128)(2,1)} %select_select_fusion), calls=%async_computation | async-start | bytes 2097152 | tf_op jit(solution)/shard_map/all_to_all | solution.py:76
  72.8 17.7 %copy-start.20 = (s32[4,5,4]{1,2,0:T(4,128)S(1)}, s32[4,5,4]{1,2,0:T(4,128)}, u32[]{:S(2)}) copy-start(s32[4,5,4]{1,2,0:T(4,128)} %param.17) | copy-start | bytes 964
  72.9 18.4 %copy-start.21 = (s32[4]{0:T(128)S(1)}, s32[4]{0:T(128)}, u32[]{:S(2)}) copy-start(s32[4]{0:T(128)} %param.13) | copy-start | bytes 52
  72.9 31.5 %copy-start.24 = (bf16[4,128]{1,0:T(4,128)(2,1)S(1)}, bf16[4,128]{1,0:T(4,128)(2,1)}, u32[]{:S(2)}) copy-start(bf16[4,128]{1,0:T(4,128)(2,1)} %param.15) | copy-start | bytes 3076
  72.9 31.6 %copy-start.22 = (f32[512]{0:T(512)S(1)}, f32[512]{0:T(512)}, u32[]{:S(2)}) copy-start(f32[512]{0:T(512)} %param.14) | copy-start | bytes 6148
  72.9 54.8 %copy-start.26 = (s32[2]{0:T(128)S(1)}, s32[2]{0:T(128)}, u32[]{:S(2)}) copy-start(s32[2]{0:T(128)} %constant.159) | copy-start | bytes 28
  91.3 2.8 collective-permute-start.26
  92.6 2.4 collective-permute-start.34
  92.9 4.6 %collective-permute-start.18 = (s32[4]{0:T(128)S(1)}, s32[4]{0:T(128)S(1)}, u32[]{:S(2)}, u32[]{:S(2)}) collective-permute-start(s32[4]{0:T(128)S(1)} %get-tuple-element.59), channel_id=1, source_target_pairs={{0,32},{16,48},{32,0},{48,16},{64,96},{80,112},{96,64},{112,80},{1... | collective-permute-start | bytes 56 | tf_op jit(solution)/shard_map/ppermute | solution.py:18
  94.1 3.9 collective-permute-start.10
  95.0 5.4 %collective-permute-start.27 = (s32[4]{0:T(128)S(1)}, s32[4]{0:T(128)S(1)}, u32[]{:S(2)}, u32[]{:S(2)}) collective-permute-start(s32[4]{0:T(128)S(1)} %broadcast_select_fusion.27), channel_id=1, source_target_pairs={{0,64},{16,80},{32,96},{48,112},{64,0},{80,16},{96,32},{112,48},{1... | collective-permute-start | bytes 56 | tf_op jit(solution)/shard_map/ppermute | solution.py:18
  97.5 3.9 collective-permute-start.35
  98.0 3.9 collective-permute-start.19
  100.5 3.9 collective-permute-start.11
  104.4 3.4 collective-permute-start.32
  104.7 4.0 collective-permute-start.24
  106.3 4.6 %collective-permute-start.16 = (bf16[4,128]{1,0:T(4,128)(2,1)S(1)}, bf16[4,128]{1,0:T(4,128)(2,1)S(1)}, u32[]{:S(2)}, u32[]{:S(2)}) collective-permute-start(bf16[4,128]{1,0:T(4,128)(2,1)S(1)} %get-tuple-element.50), channel_id=1, source_target_pairs={{0,32},{16,48},{32,0},{48,16},{64,96},{80,112},{96,64},{112,80},{1... | collective-permute-start | bytes 3080 | tf_op jit(solution)/shard_map/ppermute | solution.py:18
  106.4 5.5 %collective-permute-start.7 = (bf16[4,128]{1,0:T(4,128)(2,1)S(1)}, bf16[4,128]{1,0:T(4,128)(2,1)S(1)}, u32[]{:S(2)}, u32[]{:S(2)}) collective-permute-start(bf16[4,128]{1,0:T(4,128)(2,1)S(1)} %get-tuple-element.51), channel_id=1, source_target_pairs={{0,32},{16,48},{32,0},{48,16},{64,96},{80,112},{96,64},{112,80},{1... | collective-permute-start | bytes 3080 | tf_op jit(solution)/shard_map/ppermute | solution.py:18
  107.7 6.3 %collective-permute-start.33 = (bf16[4,128]{1,0:T(4,128)(2,1)S(1)}, bf16[4,128]{1,0:T(4,128)(2,1)S(1)}, u32[]{:S(2)}, u32[]{:S(2)}) collective-permute-start(bf16[4,128]{1,0:T(4,128)(2,1)S(1)} %broadcast_select_fusion.25), channel_id=1, source_target_pairs={{0,64},{16,80},{32,96},{48,112},{64,0},{80,16},{96,32},{112,48},{1... | collective-permute-start | bytes 3080 | tf_op jit(solution)/shard_map/ppermute | solution.py:18
  108.7 5.3 %collective-permute-start.25 = (bf16[4,128]{1,0:T(4,128)(2,1)S(1)}, bf16[4,128]{1,0:T(4,128)(2,1)S(1)}, u32[]{:S(2)}, u32[]{:S(2)}) collective-permute-start(bf16[4,128]{1,0:T(4,128)(2,1)S(1)} %broadcast_select_fusion.30), channel_id=1, source_target_pairs={{0,64},{16,80},{32,96},{48,112},{64,0},{80,16},{96,32},{112,48},{1... | collective-permute-start | bytes 3080 | tf_op jit(solution)/shard_map/ppermute | solution.py:18
  110.9 4.0 %collective-permute-start.17 = (bf16[4,128]{1,0:T(4,128)(2,1)S(1)}, bf16[4,128]{1,0:T(4,128)(2,1)S(1)}, u32[]{:S(2)}, u32[]{:S(2)}) collective-permute-start(bf16[4,128]{1,0:T(4,128)(2,1)S(1)} %broadcast_select_fusion.35), channel_id=1, source_target_pairs={{0,64},{16,80},{32,96},{48,112},{64,0},{80,16},{96,32},{112,48},{1... | collective-permute-start | bytes 3080 | tf_op jit(solution)/shard_map/ppermute | solution.py:18
  111.9 4.0 %collective-permute-start.8 = (bf16[4,128]{1,0:T(4,128)(2,1)S(1)}, bf16[4,128]{1,0:T(4,128)(2,1)S(1)}, u32[]{:S(2)}, u32[]{:S(2)}) collective-permute-start(bf16[4,128]{1,0:T(4,128)(2,1)S(1)} %broadcast_select_fusion.40), channel_id=1, source_target_pairs={{0,64},{16,80},{32,96},{48,112},{64,0},{80,16},{96,32},{112,48},{1... | collective-permute-start | bytes 3080 | tf_op jit(solution)/shard_map/ppermute | solution.py:18
  114.9 3.0 collective-permute-start.20
  115.9 4.5 %collective-permute-start.28 = (s32[4,512]{1,0:T(4,128)S(1)}, s32[4,512]{1,0:T(4,128)S(1)}, u32[]{:S(2)}, u32[]{:S(2)}) collective-permute-start(s32[4,512]{1,0:T(4,128)S(1)} %get-tuple-element.32), channel_id=1, source_target_pairs={{0,32},{16,48},{32,0},{48,16},{64,96},{80,112},{96,64},{112,80},{1... | collective-permute-start | bytes 24584 | tf_op jit(solution)/shard_map/ppermute | solution.py:18
  116.5 4.6 %collective-permute-start.12 = (s32[4,512]{1,0:T(4,128)S(1)}, s32[4,512]{1,0:T(4,128)S(1)}, u32[]{:S(2)}, u32[]{:S(2)}) collective-permute-start(s32[4,512]{1,0:T(4,128)S(1)} %get-tuple-element.33), channel_id=1, source_target_pairs={{0,32},{16,48},{32,0},{48,16},{64,96},{80,112},{96,64},{112,80},{1... | collective-permute-start | bytes 24584 | tf_op jit(solution)/shard_map/ppermute | solution.py:18
  117.4 6.2 %collective-permute-start.1 = (s32[4,512]{1,0:T(4,128)S(1)}, s32[4,512]{1,0:T(4,128)S(1)}, u32[]{:S(2)}, u32[]{:S(2)}) collective-permute-start(s32[4,512]{1,0:T(4,128)S(1)} %get-tuple-element.34), channel_id=1, source_target_pairs={{0,32},{16,48},{32,0},{48,16},{64,96},{80,112},{96,64},{112,80},{1... | collective-permute-start | bytes 24584 | tf_op jit(solution)/shard_map/ppermute | solution.py:18
  118.0 6.3 %collective-permute-start.21 = (s32[4,512]{1,0:T(4,128)S(1)}, s32[4,512]{1,0:T(4,128)S(1)}, u32[]{:S(2)}, u32[]{:S(2)}) collective-permute-start(s32[4,512]{1,0:T(4,128)S(1)} %broadcast_select_fusion.16), channel_id=1, source_target_pairs={{0,64},{16,80},{32,96},{48,112},{64,0},{80,16},{96,32},{112,48},{1... | collective-permute-start | bytes 24584 | tf_op jit(solution)/shard_map/ppermute | solution.py:18
  120.4 4.1 %collective-permute-start.29 = (s32[4,512]{1,0:T(4,128)S(1)}, s32[4,512]{1,0:T(4,128)S(1)}, u32[]{:S(2)}, u32[]{:S(2)}) collective-permute-start(s32[4,512]{1,0:T(4,128)S(1)} %broadcast_select_fusion.14), channel_id=1, source_target_pairs={{0,64},{16,80},{32,96},{48,112},{64,0},{80,16},{96,32},{112,48},{1... | collective-permute-start | bytes 24584 | tf_op jit(solution)/shard_map/ppermute | solution.py:18
  121.1 4.1 %collective-permute-start.13 = (s32[4,512]{1,0:T(4,128)S(1)}, s32[4,512]{1,0:T(4,128)S(1)}, u32[]{:S(2)}, u32[]{:S(2)}) collective-permute-start(s32[4,512]{1,0:T(4,128)S(1)} %broadcast_select_fusion.18), channel_id=1, source_target_pairs={{0,64},{16,80},{32,96},{48,112},{64,0},{80,16},{96,32},{112,48},{1... | collective-permute-start | bytes 24584 | tf_op jit(solution)/shard_map/ppermute | solution.py:18
  123.6 4.1 %collective-permute-start.2 = (s32[4,512]{1,0:T(4,128)S(1)}, s32[4,512]{1,0:T(4,128)S(1)}, u32[]{:S(2)}, u32[]{:S(2)}) collective-permute-start(s32[4,512]{1,0:T(4,128)S(1)} %broadcast_select_fusion.20), channel_id=1, source_target_pairs={{0,64},{16,80},{32,96},{48,112},{64,0},{80,16},{96,32},{112,48},{1... | collective-permute-start | bytes 24584 | tf_op jit(solution)/shard_map/ppermute | solution.py:18
  136.8 8.4 %collective-permute-start.3 = (bf16[4,512,128]{1,2,0:T(8,128)(2,1)S(1)}, bf16[4,512,128]{1,2,0:T(8,128)(2,1)S(1)}, u32[]{:S(2)}, u32[]{:S(2)}) collective-permute-start(bf16[4,512,128]{1,2,0:T(8,128)(2,1)S(1)} %fusion.1), channel_id=1, source_target_pairs={{0,16},{16,0},{32,48},{48,32},{64,80},{80,64},{96,112},{112,96},{1... | collective-permute-start | bytes 1572872 | tf_op jit(solution)/shard_map/ppermute | solution.py:18
  146.6 20.3 %collective-permute-start.30 = (bf16[4,512,128]{1,2,0:T(8,128)(2,1)}, bf16[4,512,128]{1,2,0:T(8,128)(2,1)}, u32[]{:S(2)}, u32[]{:S(2)}) collective-permute-start(bf16[4,512,128]{1,2,0:T(8,128)(2,1)} %get-tuple-element.27), channel_id=1, source_target_pairs={{0,32},{16,48},{32,0},{48,16},{64,96},{80,112},{96,64},{112,80},{1... | collective-permute-start | bytes 1572872 | tf_op jit(solution)/shard_map/ppermute | solution.py:18
  160.8 10.3 %collective-permute-start.22 = (bf16[4,512,128]{1,2,0:T(8,128)(2,1)}, bf16[4,512,128]{1,2,0:T(8,128)(2,1)S(1)}, u32[]{:S(2)}, u32[]{:S(2)}) collective-permute-start(bf16[4,512,128]{1,2,0:T(8,128)(2,1)} %get-tuple-element.28), channel_id=1, source_target_pairs={{0,32},{16,48},{32,0},{48,16},{64,96},{80,112},{96,64},{112,80},{1... | collective-permute-start | bytes 1572872 | tf_op jit(solution)/shard_map/ppermute | solution.py:18
  165.4 13.6 %collective-permute-start.14 = (bf16[4,512,128]{1,2,0:T(8,128)(2,1)S(1)}, bf16[4,512,128]{1,2,0:T(8,128)(2,1)S(1)}, u32[]{:S(2)}, u32[]{:S(2)}) collective-permute-start(bf16[4,512,128]{1,2,0:T(8,128)(2,1)S(1)} %copy-done.15), channel_id=1, source_target_pairs={{0,32},{16,48},{32,0},{48,16},{64,96},{80,112},{96,64},{112,80},{1... | collective-permute-start | bytes 1572872 | tf_op jit(solution)/shard_map/ppermute | solution.py:18
  165.5 24.7 %collective-permute-start.4 = (bf16[4,512,128]{1,2,0:T(8,128)(2,1)S(1)}, bf16[4,512,128]{1,2,0:T(8,128)(2,1)S(1)}, u32[]{:S(2)}, u32[]{:S(2)}) collective-permute-start(bf16[4,512,128]{1,2,0:T(8,128)(2,1)S(1)} %copy-done.14), channel_id=1, source_target_pairs={{0,32},{16,48},{32,0},{48,16},{64,96},{80,112},{96,64},{112,80},{1... | collective-permute-start | bytes 1572872 | tf_op jit(solution)/shard_map/ppermute | solution.py:18
  168.0 35.0 %collective-permute-start.31 = (bf16[4,512,128]{1,2,0:T(8,128)(2,1)S(1)}, bf16[4,512,128]{1,2,0:T(8,128)(2,1)S(1)}, u32[]{:S(2)}, u32[]{:S(2)}) collective-permute-start(bf16[4,512,128]{1,2,0:T(8,128)(2,1)S(1)} %broadcast_select_fusion.1), channel_id=1, source_target_pairs={{0,64},{16,80},{32,96},{48,112},{64,0},{80,16},{96,32},{112,48},{1... | collective-permute-start | bytes 1572872 | tf_op jit(solution)/shard_map/ppermute | solution.py:18
  173.1 41.5 %collective-permute-start.23 = (bf16[4,512,128]{1,2,0:T(8,128)(2,1)}, bf16[4,512,128]{1,2,0:T(8,128)(2,1)}, u32[]{:S(2)}, u32[]{:S(2)}) collective-permute-start(bf16[4,512,128]{1,2,0:T(8,128)(2,1)} %broadcast_select_fusion.4), channel_id=1, source_target_pairs={{0,64},{16,80},{32,96},{48,112},{64,0},{80,16},{96,32},{112,48},{1... | collective-permute-start | bytes 1572872 | tf_op jit(solution)/shard_map/ppermute | solution.py:18
  179.8 46.0 %collective-permute-start.15 = (bf16[4,512,128]{1,2,0:T(8,128)(2,1)}, bf16[4,512,128]{1,2,0:T(8,128)(2,1)}, u32[]{:S(2)}, u32[]{:S(2)}) collective-permute-start(bf16[4,512,128]{1,2,0:T(8,128)(2,1)} %broadcast_select_fusion.7), channel_id=1, source_target_pairs={{0,64},{16,80},{32,96},{48,112},{64,0},{80,16},{96,32},{112,48},{1... | collective-permute-start | bytes 1572872 | tf_op jit(solution)/shard_map/ppermute | solution.py:18
  191.0 46.1 %collective-permute-start.5 = (bf16[4,512,128]{1,2,0:T(8,128)(2,1)}, bf16[4,512,128]{1,2,0:T(8,128)(2,1)}, u32[]{:S(2)}, u32[]{:S(2)}) collective-permute-start(bf16[4,512,128]{1,2,0:T(8,128)(2,1)} %broadcast_select_fusion.10), channel_id=1, source_target_pairs={{0,64},{16,80},{32,96},{48,112},{64,0},{80,16},{96,32},{112,48},{1... | collective-permute-start | bytes 1572872 | tf_op jit(solution)/shard_map/ppermute | solution.py:18
  286.7 6.5 %copy-start.16 = (bf16[4,4,128,128]{2,3,0,1:T(8,128)(2,1)}, bf16[4,4,128,128]{2,3,0,1:T(8,128)(2,1)S(1)}, u32[]{:S(2)}) copy-start(bf16[4,4,128,128]{2,3,0,1:T(8,128)(2,1)S(1)} %get-tuple-element.47) | copy-start | bytes 1572868
  308.5 5.5 %copy-start.12 = (f32[2048,4,128,1]{2,0,1,3:T(8,128)S(1)}, f32[2048,4,128,1]{2,0,1,3:T(8,128)}, u32[]{:S(2)}) copy-start(f32[2048,4,128,1]{2,0,1,3:T(8,128)} %fusion.31) | copy-start | bytes 12582916
  326.0 67.4 %all-to-all-start.1 = ((f32[4,2048,128]{2,0,1:T(4,128)}), f32[4,2048,128]{2,0,1:T(4,128)}, u32[]{:S(2)}, u32[]{:S(2)}) async-start(f32[4,2048,128]{2,0,1:T(4,128)} %copy.114), calls=%async_computation.1 | async-start | bytes 8388608 | tf_op jit(solution)/shard_map/all_to_all | solution.py:133
  (17 other events, 57.1 us)
where the time goes:
time: 404 us; the launch traced here: 399 us
  local copies, waits for them, and re-layouts  155 us (38%)
  waiting for transfers between devices  109 us (27%)
  starting transfers between devices  64.4 us (16%)
  matrix products  35.3 us (9%)
  other arithmetic  25 us (6%)
  between operations  9.11 us (2%)
    ppermute x36, waiting for transfers between devices, partner(): lax.ppermute(x, axis, [(i, i ^ 1 << stride) for i in range(lax.axis_size(...  66.6 us
    unnamed x73, local copies, waits for them, and re-layouts  60.4 us
    all_to_all x1, waiting for transfers between devices, per_device(): lax.all_to_all(density, 'aux', split_axis=1, concat_axis=0, tiled=True)  42.8 us
    ppermute x36, starting transfers between devices, partner(): lax.ppermute(x, axis, [(i, i ^ 1 << stride) for i in range(lax.axis_size(...  38.9 us
    gather x4, local copies, waits for them, and re-layouts, per_device(): jnp.take_along_axis(domain, where_at, axis=1)  33 us
    dot_general x5, matrix products, pair_terms(): jnp.einsum('kpa,lpb->klab', raw_full, spread_out, preferred_element_type=...  19.9 us
    gather x3, local copies, waits for them, and re-layouts, per_device(): jnp.take_along_axis(own_starts, source, axis=1)  17.6 us
    all_to_all x1, starting transfers between devices, per_device(): lax.all_to_all(density, 'aux', split_axis=1, concat_axis=0, tiled=True)  16.3 us
  transfers between devices with their start and end apart: 38, of which 16 were waited for; matrix products, arithmetic and copies ran while one was open for 28% of the time, Pallas kernels for 0%

commit v1 on v0

v1 whole, which is shorter than its diff:
```python
import functools

import jax
import jax.numpy as jnp
from jax import lax
from jax.experimental import pallas as pl
from jax.experimental.pallas import tpu as pltpu
from jax.sharding import PartitionSpec as P

PAIR_SCALE = 1.3
BF16 = jnp.bfloat16
F32 = jnp.float32
I32 = jnp.int32
NOSV = 128
NFIT = 512
OCC = 4
AUXD = 128
NAUX_DEV = 16
NAUX = AUXD * NAUX_DEV
CAP = 64
CHUNKS = NFIT // CAP
ENDS = NAUX_DEV + 1
SLAB = OCC * NOSV
VMEM_LIMIT = 50 * 1024 * 1024


def params(**kw):
    return pltpu.CompilerParams(vmem_limit_bytes=VMEM_LIMIT, **kw)


def pack_kernel(table, raw, out):
    lanes = lax.broadcasted_iota(I32, (2 * CAP, 2 * AUXD), 1)
    for pair in range(8):
        column = table[0, :, pair : pair + 1]
        pick = jnp.where(lanes == column, 1.0, 0.0).astype(BF16)
        rows = raw[2 * pair : 2 * pair + 2].reshape(2 * AUXD, NOSV)
        got = jnp.dot(pick, rows, preferred_element_type=F32).astype(BF16)
        out[2 * pair] = got[:CAP]
        out[2 * pair + 1] = got[CAP:]


def pack_rows(raw_rows, domain, run_starts, run_ends, my_aux):
    group = raw_rows.shape[0]
    start = lax.dynamic_slice_in_dim(run_starts, my_aux, 1, 1)[:, :, None]
    end = lax.dynamic_slice_in_dim(run_ends, my_aux, 1, 1)[:, :, None]
    position = jnp.arange(NFIT, dtype=I32).reshape(1, CHUNKS, CAP)
    inside = (position >= start) & (position < end)
    odd = (jnp.arange(group, dtype=I32) % 2 * AUXD)[:, None, None]
    code = domain.reshape(group, CHUNKS, CAP) + odd + 1
    table = jnp.sum(jnp.where(inside, code, 0), axis=1) - 1
    steps = group // 16
    table = table.reshape(steps, 8, 2 * CAP).transpose(0, 2, 1)
    return pl.pallas_call(
        pack_kernel,
        grid=(steps,),
        in_specs=[
            pl.BlockSpec((1, 2 * CAP, 8), lambda i: (i, 0, 0)),
            pl.BlockSpec((16, AUXD, NOSV), lambda i: (i, 0, 0)),
        ],
        out_specs=pl.BlockSpec((16, CAP, NOSV), lambda i: (i, 0, 0)),
        out_shape=jax.ShapeDtypeStruct((group, CAP, NOSV), BF16),
        compiler_params=params(),
        name="pack_rows",
    )(table, raw_rows)


def fit_kernel(ends, received, metric, fitted, block, acc):
    k = pl.program_id(0)
    acc[...] = jnp.zeros(acc.shape, F32)
    sub = lax.broadcasted_iota(I32, (CAP, NOSV), 0)
    for a in range(NAUX_DEV):
        start = ends[k * ENDS + a]
        at = pl.multiple_of(jnp.minimum(start // CAP, CHUNKS - 1) * CAP, CAP)
        first = start % CAP
        rows = received[a, 0].astype(F32)
        acc[pl.ds(at, CAP), :] += jnp.where(sub >= first, rows, 0.0)
        acc[pl.ds(at + CAP, CAP), :] += jnp.where(sub >= first, 0.0, rows)
    whole = acc[:NFIT, :].astype(BF16)
    block[0] = whole
    fitted[0] = jnp.dot(metric[0], whole, preferred_element_type=F32).astype(BF16)


def fit(ends, received, metric):
    shape = jax.ShapeDtypeStruct((OCC, NFIT, NOSV), BF16)
    return pl.pallas_call(
        fit_kernel,
        grid_spec=pltpu.PrefetchScalarGridSpec(
            num_scalar_prefetch=1,
            grid=(OCC,),
            in_specs=[
                pl.BlockSpec((NAUX_DEV, 1, CAP, NOSV), lambda k, e: (0, k, 0, 0)),
                pl.BlockSpec((1, NFIT, NFIT), lambda k, e: (k, 0, 0)),
            ],
            out_specs=[
                pl.BlockSpec((1, NFIT, NOSV), lambda k, e: (k, 0, 0)),
                pl.BlockSpec((1, NFIT, NOSV), lambda k, e: (k, 0, 0)),
            ],
            scratch_shapes=[pltpu.VMEM((NFIT + CAP, NOSV), F32)],
        ),
        out_shape=[shape, shape],
        compiler_params=params(),
        name="fit",
    )(ends, received, metric)


def spread_rows(source, slot, table_at, windows, ends, store):
    sub = lax.broadcasted_iota(I32, (AUXD, 2 * CAP), 0)
    lane = lax.broadcasted_iota(I32, (1, 2 * CAP), 1)
    for a in range(NAUX_DEV):
        start = ends[table_at * ENDS + a]
        end = ends[table_at * ENDS + a + 1]
        chunk = jnp.minimum(start // CAP, CHUNKS - 2)
        at = pl.multiple_of(chunk * CAP, CAP)
        row = windows[table_at, pl.ds(chunk, 1), :]
        row = jnp.where((lane >= start - at) & (lane < end - at), row, -1)
        pick = jnp.where(sub == row, 1.0, 0.0).astype(BF16)
        rows = source[slot, pl.ds(at, 2 * CAP), :]
        store(a, jnp.dot(pick, rows, preferred_element_type=F32))


def one_round(
    q, table0, source, ends, screen, windows, far_energy, own_energy, raw_t, spread, ints, amps, den, energy, first
):
    for l in range(OCC):

        def store(a, value, l=l):
            spread[a * AUXD : (a + 1) * AUXD, l * NOSV : (l + 1) * NOSV] = value.astype(BF16)

        spread_rows(source, l, table0 + l, windows, ends, store)
    ints[...] = jnp.dot(raw_t[...], spread[...], preferred_element_type=F32)
    for k in range(OCC):
        for l in range(OCC):
            ks = slice(k * NOSV, (k + 1) * NOSV)
            ls = slice(l * NOSV, (l + 1) * NOSV)
            value = ints[ks, ls]
            denominator = own_energy[ks, :] + far_energy[pl.ds(table0 + l, 1), :]
            amp = (screen[(k * 5 + q) * OCC + l] * value / denominator).astype(BF16)
            amps[ks, ls] = amp
            part = jnp.sum(amp.astype(F32) * value, axis=0, keepdims=True)
            energy[q, k * OCC + l : k * OCC + l + 1, :] = part
    tile = 512
    for m in range(NAUX // tile):
        ms = slice(m * tile, (m + 1) * tile)
        value = lax.dot_general(
            spread[ms, :], amps[...], (((1,), (1,)), ((), ())), preferred_element_type=F32
        )
        den[ms, :] = value if first else den[ms, :] + value


def own_kernel(
    ends, screen, windows, far_energy, own_energy, block, fitted, raw_out, den_out, energy,
    spread, ints, amps, sems,
):
    for k in range(OCC):

        def store(a, value, k=k):
            raw_out[k * NOSV : (k + 1) * NOSV, a * AUXD : (a + 1) * AUXD] = value.T.astype(BF16)

        spread_rows(block, k, k, windows, ends, store)
    energy[...] = jnp.zeros(energy.shape, F32)
    one_round(
        0, 0, fitted, ends, screen, windows, far_energy, own_energy, raw_out, spread, ints, amps, den_out, energy, True
    )


def own_round(ends, screen, windows, far_energy, own_energy, block, fitted):
    smem = pl.BlockSpec(memory_space=pltpu.SMEM)
    vmem = pl.BlockSpec(memory_space=pltpu.VMEM)
    return pl.pallas_call(
        own_kernel,
        in_specs=[smem, smem] + [vmem] * 5,
        out_specs=[vmem] * 3,
        out_shape=[
            jax.ShapeDtypeStruct((SLAB, NAUX), BF16),
            jax.ShapeDtypeStruct((NAUX, SLAB), F32),
            jax.ShapeDtypeStruct((5, 16, NOSV), F32),
        ],
        scratch_shapes=[
            pltpu.VMEM((NAUX, SLAB), BF16),
            pltpu.VMEM((SLAB, SLAB), F32),
            pltpu.VMEM((SLAB, SLAB), BF16),
            pltpu.SemaphoreType.DMA((2,)),
        ],
        compiler_params=params(),
        name="own_round",
    )(ends, screen, windows, far_energy, own_energy, block, fitted)


def phase_kernel(
    masks, last, pieces, rounds, ends, screen, windows, far_energy, own_energy, raw_in, den_in, *rest
):
    far = rest[: len(pieces)]
    den_out, energy, raw_t, den, source, spread, ints, amps, sems = rest[len(pieces) :]

    def wanted(mask):
        found = mask == masks[0]
        for other in masks[1:]:
            found |= mask == other
        return found

    count = wanted(rounds[0]).astype(I32)
    for q in range(1, 4):
        count += wanted(rounds[q]).astype(I32)
    energy[...] = jnp.zeros(energy.shape, F32)

    load_den = pltpu.make_async_copy(den_in, den, sems.at[0])
    load_raw = pltpu.make_async_copy(raw_in, raw_t, sems.at[1])

    def work():
        load_den.start()
        load_raw.start()
        load_den.wait()
        load_raw.wait()

        def body(q, carry):
            mask = rounds[q]

            @pl.when(wanted(mask))
            def _():
                for mask_at, piece_list in zip(masks, pieces_of(pieces, masks)):

                    @pl.when(mask == mask_at)
                    def _(piece_list=piece_list):
                        for index, lo, hi in piece_list:
                            copy = pltpu.make_async_copy(far[index], source.at[pl.ds(lo, hi - lo)], sems.at[2])
                            copy.start()
                            copy.wait()

                one_round(
                    q + 1, rounds[4 + q] * OCC, source, ends, screen, windows, far_energy, own_energy,
                    raw_t, spread, ints, amps, den, energy, False,
                )

            return carry

        lax.fori_loop(0, 4, body, 0)

    if last:
        work()
        for a in range(NAUX_DEV):
            for k in range(OCC):
                den_out[a, k] = den[a * AUXD : (a + 1) * AUXD, k * NOSV : (k + 1) * NOSV].astype(BF16)
    else:

        @pl.when(count > 0)
        def _():
            work()
            save = pltpu.make_async_copy(den, den_out, sems.at[0])
            save.start()
            save.wait()


def pieces_of(pieces, masks):
    return [[p[1:] for p in pieces_entry(pieces) if p[0] == mask] for mask in masks]


def pieces_entry(pieces):
    return [(mask, index, lo, hi) for index, (mask, lo, hi) in enumerate(pieces)]


def phase(masks, last, pieces, rounds, ends, screen, windows, far_energy, own_energy, raw_t, den, far):
    smem = pl.BlockSpec(memory_space=pltpu.SMEM)
    vmem = pl.BlockSpec(memory_space=pltpu.VMEM)
    hbm = pl.BlockSpec(memory_space=pl.ANY)
    if last:
        den_shape = jax.ShapeDtypeStruct((NAUX_DEV, OCC, AUXD, NOSV), BF16)
        den_spec = vmem
        alias = {}
    else:
        den_shape = jax.ShapeDtypeStruct((NAUX, SLAB), F32)
        den_spec = hbm
        alias = {7: 0}
    return pl.pallas_call(
        functools.partial(phase_kernel, masks, last, pieces),
        in_specs=[smem, smem, smem, vmem, vmem, vmem, hbm, hbm] + [hbm] * len(far),
        out_specs=[den_spec, vmem],
        out_shape=[den_shape, jax.ShapeDtypeStruct((5, 16, NOSV), F32)],
        scratch_shapes=[
            pltpu.VMEM((SLAB, NAUX), BF16),
            pltpu.VMEM((NAUX, SLAB), F32),
            pltpu.VMEM((OCC, NFIT, NOSV), BF16),
            pltpu.VMEM((NAUX, SLAB), BF16),
            pltpu.VMEM((SLAB, SLAB), F32),
            pltpu.VMEM((SLAB, SLAB), BF16),
            pltpu.SemaphoreType.DMA((3,)),
        ],
        input_output_aliases=alias,
        compiler_params=params(),
        name="phase_" + "_".join(str(m) for m in masks),
    )(rounds, ends, screen, windows, far_energy, own_energy, raw_t, den, *far)


def tables(meta):
    n = meta.shape[0]
    slots = meta.reshape(n * OCC, 8, NOSV)
    dom = slots[:, :4].reshape(n * OCC, CHUNKS, CAP).astype(I32)
    after = jnp.concatenate([dom[:, 1:], dom[:, :1]], axis=1)
    windows = jnp.concatenate([dom, after], axis=2)
    counts = slots[:, 4, :NAUX_DEV]
    below = jnp.arange(NAUX_DEV)[None, :] < jnp.arange(ENDS)[:, None]
    ends = jnp.sum(jnp.where(below[None], counts[:, None, :], 0.0), axis=2).astype(I32)
    return windows, ends.reshape(-1), slots[:, 5] - slots[:, 6]


def flip(x, mask):
    return lax.ppermute(x, "orb", [(i, i ^ mask) for i in range(lax.axis_size("orb"))])


def per_device(
    raw_rows, fit_metric, domain, counts, orbital_ids, occ_energy, osv_energy, matchings, screening
):
    my_aux = lax.axis_index("aux")
    my_orb = lax.axis_index("orb")
    group = raw_rows.shape[0]
    own_domain = lax.dynamic_slice_in_dim(domain, my_aux * OCC, OCC, 0)
    own_counts = lax.dynamic_slice_in_dim(counts, my_aux * OCC, OCC, 0)
    everyone = jnp.arange(occ_energy.shape[0], dtype=I32)
    own_occ = jnp.sum(
        jnp.where(orbital_ids[:, None] == everyone[None, :], occ_energy[None, :], 0.0), axis=1
    )
    own_osv = osv_energy.astype(F32)
    meta = jnp.concatenate(
        [
            own_domain.astype(F32).reshape(OCC, 4, NOSV),
            jnp.pad(own_counts.astype(F32), ((0, 0), (0, NOSV - NAUX_DEV)))[:, None, :],
            own_osv[:, None, :],
            jnp.broadcast_to(own_occ[:, None, None], (OCC, 2, NOSV)),
        ],
        axis=1,
    )
    everywhere = lax.all_gather(meta, "orb", axis=0)
    own_windows, own_ends, own_term = tables(meta[None])
    windows, ends, far_energy = tables(everywhere)
    own_energy = jnp.broadcast_to(own_term.reshape(SLAB, 1), (SLAB, NOSV))
    screen = screening.astype(F32).reshape(-1)
    rounds = jnp.concatenate(
        [matchings[:, 0], lax.dynamic_index_in_dim(matchings, my_orb, 1, keepdims=False)]
    )

    upto = jnp.arange(NAUX_DEV)[None, :] <= jnp.arange(NAUX_DEV)[:, None]
    run_ends = jnp.sum(jnp.where(upto[None], counts[:, None, :], 0), axis=2)
    packed = pack_rows(raw_rows, domain, run_ends - counts, run_ends, my_aux)
    packed = packed.reshape(NAUX_DEV, OCC, CAP, NOSV)
    received = lax.all_to_all(packed, "aux", split_axis=0, concat_axis=0, tiled=True)
    fitted, block = fit(own_ends, received, fit_metric)

    far1, far2, far6 = flip(fitted, 1), flip(fitted, 2), flip(fitted, 6)
    raw_t, den, energy0 = own_round(
        own_ends, screen, own_windows, own_term, own_energy, block, fitted
    )
    far3, far4, far7 = flip(far2, 1), flip(far6, 2), flip(far1, 6)
    common = (rounds, ends, screen, windows, far_energy, own_energy, raw_t)
    den, energy1 = phase(
        (1, 2, 6), False, ((1, 0, 4), (2, 0, 4), (6, 0, 4)), *common, den, (far1, far2, far6)
    )
    far5 = (flip(far4[0:1], 1), flip(far7[1:2], 2), flip(far3[2:4], 6))
    den, energy2 = phase(
        (3, 4, 7), False, ((3, 0, 4), (4, 0, 4), (7, 0, 4)), *common, den, (far3, far4, far7)
    )
    sent, energy3 = phase((5,), True, ((5, 0, 1), (5, 1, 2), (5, 2, 4)), *common, den, far5)
    returned = lax.all_to_all(sent, "aux", split_axis=0, concat_axis=0, tiled=True)
    density = returned.reshape(group, AUXD, NOSV).astype(F32)
    total = jnp.sum(energy0 + energy1 + energy2 + energy3, axis=2)
    energies = total.reshape(5, OCC, OCC).transpose(1, 0, 2) * (PAIR_SCALE / (NOSV * NOSV))
    return density, energies


def solution(mesh):
    placed = (
        P("orb", "aux", None),
        P(("orb", "aux"), None, None),
        P("orb", None),
        P("orb", None),
        P(("orb", "aux")),
        P(),
        P(("orb", "aux"), None),
        P(),
        P(("orb", "aux"), None, None),
    )
    return jax.shard_map(
        per_device,
        mesh=mesh,
        in_specs=placed,
        out_specs=(P("orb", "aux", None), P(("orb", "aux"), None, None)),
        check_vma=False,
    )
```

time: 404 us -> 187 us (0.46)
  local copies, waits for them, and re-layouts: 155 us -> 26.5 us
  waiting for transfers between devices: 109 us -> 38.5 us
  Pallas kernels: 0 us -> 40.5 us
  matrix products: 35.3 us -> 0 us
  starting transfers between devices: 64.4 us -> 35.7 us
  blocking collectives: 0 us -> 28.5 us
  other arithmetic: 25 us -> 14.1 us
  between operations: 9.11 us -> 0.99 us
    gather x9 -> x0, local copies, waits for them, and re-layouts: 68.9 us -> none  [the longest x4 33 us: per_device(): jnp.take_along_axis(domain, where_at, axis=1)]
    ppermute x36 -> x9, waiting for transfers between devices: 66.6 us -> 10.8 us  [flip(): lax.ppermute(x, 'orb', [(i, i ^ mask) for i in range(lax.axis_size('orb'))])]
    unnamed x73 -> x50, local copies, waits for them, and re-layouts: 60.4 us -> 11.5 us
    pallas_call x0 -> x6, Pallas kernels: none -> 40.5 us  [the longest x3 26.9 us: phase(): pl.pallas_call(functools.partial(phase_kernel, masks, last, pieces), in_s...]
    dot_general x11 -> x0, matrix products: 35.3 us -> none  [the longest x5 19.9 us: pair_terms(): jnp.einsum('kpa,lpb->klab', raw_full, spread_out, preferred_element_type=...]
    all_gather x0 -> x1, blocking collectives: none -> 28.5 us  [per_device(): everywhere = lax.all_gather(meta, 'orb', axis=0)]
    ppermute x36 -> x9, starting transfers between devices: 38.9 us -> 11 us  [flip(): lax.ppermute(x, 'orb', [(i, i ^ mask) for i in range(lax.axis_size('orb'))])]
    select_n x31 -> x0, other arithmetic: 15.7 us -> none  [the longest x28 12.8 us: per_device(): jnp.where(take_swap, arrived, unchanged)]
  transfers between devices with their start and end apart: 38 -> 11, of which waited for: 16 -> 4; matrix products, arithmetic and copies ran while one was open for 28% -> 12% of each run, Pallas kernels for 0% -> 11%
where the time goes in v1:
time: 187 us; the launch traced here: 185 us
  Pallas kernels  40.5 us (22%)
  waiting for transfers between devices  38.5 us (21%)
  starting transfers between devices  35.7 us (19%)
  blocking collectives  28.5 us (15%)
  local copies, waits for them, and re-layouts  26.5 us (14%)
  other arithmetic  14.1 us (8%)
    all_gather x1, blocking collectives, per_device(): everywhere = lax.all_gather(meta, 'orb', axis=0)  28.5 us
    all_to_all x1, waiting for transfers between devices, per_device(): lax.all_to_all(sent, 'aux', split_axis=0, concat_axis=0, tiled=True)  27.7 us
    pallas_call x3, Pallas kernels, phase(): pl.pallas_call(functools.partial(phase_kernel, masks, last, pieces), in_s...  26.9 us
    all_to_all x1, starting transfers between devices, per_device(): lax.all_to_all(sent, 'aux', split_axis=0, concat_axis=0, tiled=True)  15.2 us
    unnamed x50, local copies, waits for them, and re-layouts  11.5 us
    ppermute x9, starting transfers between devices, flip(): lax.ppermute(x, 'orb', [(i, i ^ mask) for i in range(lax.axis_size('orb'))])  11 us
    ppermute x9, waiting for transfers between devices, flip(): lax.ppermute(x, 'orb', [(i, i ^ mask) for i in range(lax.axis_size('orb'))])  10.8 us
    all_to_all x1, starting transfers between devices, per_device(): lax.all_to_all(packed, 'aux', split_axis=0, concat_axis=0, tiled=True)  9.46 us
  transfers between devices with their start and end apart: 11, of which 4 were waited for; matrix products, arithmetic and copies ran while one was open for 12% of the time, Pallas kernels for 11%

profile of v1, /device:TPU:1, one launch (start us, length us, event | category | flops | bytes accessed | tf_op | source)
XLA Modules:
  0.0 184.8 jit_solution(15790302243123487853)
XLA Ops:
  0.7 1.0 reshape.108
  1.7 0.8 select_reduce_fusion.2
  2.5 0.7 fusion.1
  3.7 1.6 copy-done.1
  5.3 2.6 %pack_rows.1 = bf16[64,64,128]{2,1,0:T(8,128)(2,1)} custom-call(s32[4,128,8]{2,1,0:T(8,128)S(1)} %bitcast.23, bf16[64,128,128]{2,1,0:T(8,128)(2,1)S(1)} %copy-done.1), custom_call_target="tpu_custom_call" | custom-call | tf_op jit(solution)/shard_map/pack_rows/pallas_call | solution.py:53
  8.0 9.5 %all-to-all-start = ((bf16[16,4,64,128]{3,2,1,0:T(8,128)(2,1)}), bf16[16,4,64,128]{3,2,1,0:T(8,128)(2,1)S(1)}, u32[]{:S(2)}, u32[]{:S(2)}) async-start(bf16[16,4,64,128]{3,2,1,0:T(8,128)(2,1)} %bitcast.10), calls=%async_computation | async-start | bytes 2097152 | tf_op jit(solution)/shard_map/all_to_all | solution.py:344
  17.4 0.7 fusion.5
  19.1 28.5 %all-gather = f32[32,8,128]{2,1,0:T(8,128)S(1)} all-gather(f32[4,8,128]{2,1,0:T(8,128)S(1)} %pad_maximum_fusion), channel_id=2, replica_groups=mesh['orb'=8,'aux'=16] {'orb'}, dimensions={0}, use_global_device_ids=true | all-gather | bytes 147456 | tf_op jit(solution)/shard_map/all_gather | solution.py:331
  47.7 4.1 %fit.1 = (bf16[4,512,128]{2,1,0:T(8,128)(2,1)S(1)}, bf16[4,512,128]{2,1,0:T(8,128)(2,1)S(1)}) custom-call(s32[68]{0:T(128)S(1)} %convert_element_type.55.ends, bf16[16,4,64,128]{3,2,1,0:T(8,128)(2,1)S(1)} %all-to-all-done.received, bf16[4,512,512]{2,1,0:T(8,128)(2,1)} %metric.1), custom_call_target="tpu_custom_call" | custom-call | tf_op jit(solution)/shard_map/fit/pallas_call | solution.py:85
  51.8 0.8 copy-done.4
  52.6 0.7 select_reduce_fusion.1
  53.4 1.2 collective-permute-start
  54.5 2.4 %collective-permute-start.2 = (bf16[4,512,128]{2,1,0:T(8,128)(2,1)S(1)}, bf16[4,512,128]{2,1,0:T(8,128)(2,1)S(1)}, u32[]{:S(2)}, u32[]{:S(2)}) collective-permute-start(bf16[4,512,128]{2,1,0:T(8,128)(2,1)S(1)} %get-tuple-element.14.fitted), channel_id=1, source_target_pairs={{0,96},{16,112},{32,64},{48,80},{64,32},{80,48},{96,0},{112,16},{1... | collective-permute-start | bytes 1572872 | tf_op jit(solution)/shard_map/ppermute | solution.py:306
  56.9 0.8 copy-done.2
  57.8 2.9 %collective-permute-done.1.rest_1_ = bf16[4,512,128]{2,1,0:T(8,128)(2,1)S(1)} collective-permute-done((bf16[4,512,128]{2,1,0:T(8,128)(2,1)S(1)}, bf16[4,512,128]{2,1,0:T(8,128)(2,1)S(1)}, u32[]{:S(2)}, u32[]{:S(2)}) %collective-permute-start.1) | collective-permute-done | bytes 524320 | tf_op jit(solution)/shard_map/ppermute | solution.py:306
  60.7 1.2 collective-permute-start.3
  62.5 1.3 collective-permute-done.2.rest_2_
  63.8 0.9 collective-permute-start.4
  64.6 2.1 %collective-permute-start.5 = (bf16[4,512,128]{2,1,0:T(8,128)(2,1)S(1)}, bf16[4,512,128]{2,1,0:T(8,128)(2,1)S(1)}, u32[]{:S(2)}, u32[]{:S(2)}) collective-permute-start(bf16[4,512,128]{2,1,0:T(8,128)(2,1)S(1)} %collective-permute-done.rest_0_), channel_id=1, source_target_pairs={{0,96},{16,112},{32,64},{48,80},{64,32},{80,48},{96,0},{112,16},{1... | collective-permute-start | bytes 1572872 | tf_op jit(solution)/shard_map/ppermute | solution.py:306
  68.0 6.6 %collective-permute-done.3.rest_0_ = bf16[4,512,128]{2,1,0:T(8,128)(2,1)S(1)} collective-permute-done((bf16[4,512,128]{2,1,0:T(8,128)(2,1)S(1)}, bf16[4,512,128]{2,1,0:T(8,128)(2,1)S(1)}, u32[]{:S(2)}, u32[]{:S(2)}) %collective-permute-start.3) | collective-permute-done | bytes 524320 | tf_op jit(solution)/shard_map/ppermute | solution.py:306
  74.6 0.7 slice.64
  75.4 1.6 collective-permute-start.8
  77.8 1.7 collective-permute-start.6
  80.9 1.6 convert_element_type.53
  82.5 1.6 slice.55
  84.0 1.5 slice.56
  85.5 1.3 convert_element_type.51
  86.8 1.4 copy.36
  88.2 1.3 reshape.104.screen
  89.6 1.3 convert_element_type.49
  90.9 1.4 copy.35
  92.3 1.4 convert_element_type.50.ends
  93.7 1.1 add_add_fusion.windows
  94.8 0.8 broadcast_in_dim.125.own_energy
  95.6 1.0 copy-done.3
  96.6 1.0 copy-done.5
  97.7 0.7 copy-done.7
  99.7 0.7 copy-done.18
  100.4 6.7 %own_round.1 = (bf16[512,2048]{1,0:T(8,128)(2,1)S(1)}, f32[2048,512]{1,0:T(8,128)}, f32[5,16,128]{2,1,0:T(8,128)S(1)}) custom-call(s32[68]{0:T(128)S(1)} %copy-done.18, f32[80]{0:T(128)S(1)} %copy-done.12, s32[4,8,128]{2,1,0:T(8,128)S(1)} %copy-done.7, f32[4,128]{1,0:T(4,128)S(1)} %copy-done.14, f32[512,128]{1,0:T(8,128)S(1)} %broadcast_in_dim.125.own_energy, ...), custom_call_target="tpu_custom_call" | custom-call | tf_op jit(solution)/shard_map/own_round/pallas_call | solution.py:169
  107.1 1.3 copy-done
  108.4 0.7 copy-done.6
  109.8 0.8 phase_1_2_6.1
  110.7 12.3 %phase_3_4_7.1 = (f32[2048,512]{1,0:T(8,128)}, f32[5,16,128]{2,1,0:T(8,128)S(1)}) custom-call(s32[8]{0:T(128)S(1)} %copy-done.16, s32[544]{0:T(1024)S(1)} %copy-done.6, f32[80]{0:T(128)S(1)} %copy-done.12, s32[32,8,128]{2,1,0:T(8,128)S(1)} %add_add_fusion.windows, f32[32,128]{1,0:T(8,128)S(1)} %subtract_bitcast_fusion.far_energy, ...), custom_call_target="tpu_custom_call", output_to_operand_aliasing={{0}: (7, {})} | custom-call | tf_op jit(solution)/shard_map/phase_3_4_7/pallas_call | solution.py:273
  123.0 13.8 %phase_5.1 = (bf16[16,4,128,128]{3,2,1,0:T(8,128)(2,1)}, f32[5,16,128]{2,1,0:T(8,128)S(1)}) custom-call(s32[8]{0:T(128)S(1)} %copy-done.16, s32[544]{0:T(1024)S(1)} %copy-done.6, f32[80]{0:T(128)S(1)} %copy-done.13, s32[32,8,128]{2,1,0:T(8,128)S(1)} %add_add_fusion.windows, f32[32,128]{1,0:T(8,128)S(1)} %subtract_bitcast_fusion.far_energy, ...), custom_call_target="tpu_custom_call" | custom-call | tf_op jit(solution)/shard_map/phase_5/pallas_call | solution.py:273
  136.9 15.2 %all-to-all-start.1 = ((bf16[16,4,128,128]{3,2,1,0:T(8,128)(2,1)}), bf16[16,4,128,128]{3,2,1,0:T(8,128)(2,1)}, u32[]{:S(2)}, u32[]{:S(2)}) async-start(bf16[16,4,128,128]{3,2,1,0:T(8,128)(2,1)} %get-tuple-element.19), calls=%async_computation.1 | async-start | bytes 4194304 | tf_op jit(solution)/shard_map/all_to_all | solution.py:361
  152.3 0.7 copy.40
  153.0 27.7 %all-to-all-done.1 = bf16[16,4,128,128]{3,2,1,0:T(8,128)(2,1)} async-done(((bf16[16,4,128,128]{3,2,1,0:T(8,128)(2,1)}), bf16[16,4,128,128]{3,2,1,0:T(8,128)(2,1)}, u32[]{:S(2)}, u32[]{:S(2)}) %all-to-all-start.1) | async-done | bytes 2097184 | tf_op jit(solution)/shard_map/all_to_all | solution.py:361
  180.7 4.1 %bitcast_convert_fusion = f32[64,128,128]{2,1,0:T(8,128)} fusion(bf16[16,4,128,128]{3,2,1,0:T(8,128)(2,1)} %all-to-all-done.1), kind=kLoop, calls=%fused_computation | loop fusion | flops 1048576 | bytes 6291456 | tf_op jit(solution)/shard_map/convert_element_type | solution.py:362
  (86 shorter events, 7.8 us)
Async XLA Ops:
  3.7 1.6 copy-start.1
  5.3 12.9 %copy-start.19 = (s32[64,16]{0,1:T(8,128)S(1)}, s32[64,16]{0,1:T(8,128)}, u32[]{:S(2)}) copy-start(s32[64,16]{0,1:T(8,128)} %param.12) | copy-start | bytes 12292
  5.3 13.4 %copy-start.21 = (bf16[4,128]{1,0:T(4,128)(2,1)S(1)}, bf16[4,128]{1,0:T(4,128)(2,1)}, u32[]{:S(2)}) copy-start(bf16[4,128]{1,0:T(4,128)(2,1)} %param.15) | copy-start | bytes 3076
  5.3 13.4 %copy-start.22 = (f32[512]{0:T(512)S(1)}, f32[512]{0:T(512)}, u32[]{:S(2)}) copy-start(f32[512]{0:T(512)} %param.14) | copy-start | bytes 6148
  5.3 13.4 %copy-start.23 = (s32[4]{0:T(128)S(1)}, s32[4]{0:T(128)}, u32[]{:S(2)}) copy-start(s32[4]{0:T(128)} %param.13) | copy-start | bytes 52
  8.0 39.7 %all-to-all-start = ((bf16[16,4,64,128]{3,2,1,0:T(8,128)(2,1)}), bf16[16,4,64,128]{3,2,1,0:T(8,128)(2,1)S(1)}, u32[]{:S(2)}, u32[]{:S(2)}) async-start(bf16[16,4,64,128]{3,2,1,0:T(8,128)(2,1)} %bitcast.10), calls=%async_computation | async-start | bytes 2097152 | tf_op jit(solution)/shard_map/all_to_all | solution.py:344
  18.7 33.1 %copy-start.17 = (s32[68]{0:T(128)}, s32[68]{0:T(128)S(1)}, u32[]{:S(2)}) copy-start(s32[68]{0:T(128)S(1)} %convert_element_type.55.ends) | copy-start | bytes 820
  19.1 57.9 %copy-start.20 = (s32[4,8]{1,0:T(4,128)S(1)}, s32[4,8]{1,0:T(4,128)}, u32[]{:S(2)}) copy-start(s32[4,8]{1,0:T(4,128)} %param.16) | copy-start | bytes 388
  51.8 0.8 copy-start.4
  52.6 8.0 %collective-permute-start.1 = (bf16[4,512,128]{2,1,0:T(8,128)(2,1)S(1)}, bf16[4,512,128]{2,1,0:T(8,128)(2,1)S(1)}, u32[]{:S(2)}, u32[]{:S(2)}) collective-permute-start(bf16[4,512,128]{2,1,0:T(8,128)(2,1)S(1)} %get-tuple-element.14.fitted), channel_id=1, source_target_pairs={{0,32},{16,48},{32,0},{48,16},{64,96},{80,112},{96,64},{112,80},{1... | collective-permute-start | bytes 1572872 | tf_op jit(solution)/shard_map/ppermute | solution.py:306
  53.4 11.3 %collective-permute-start = (bf16[4,512,128]{2,1,0:T(8,128)(2,1)S(1)}, bf16[4,512,128]{2,1,0:T(8,128)(2,1)S(1)}, u32[]{:S(2)}, u32[]{:S(2)}) collective-permute-start(bf16[4,512,128]{2,1,0:T(8,128)(2,1)S(1)} %get-tuple-element.14.fitted), channel_id=1, source_target_pairs={{0,16},{16,0},{32,48},{48,32},{64,80},{80,64},{96,112},{112,96},{1... | collective-permute-start | bytes 1572872 | tf_op jit(solution)/shard_map/ppermute | solution.py:306
  54.5 9.2 %collective-permute-start.2 = (bf16[4,512,128]{2,1,0:T(8,128)(2,1)S(1)}, bf16[4,512,128]{2,1,0:T(8,128)(2,1)S(1)}, u32[]{:S(2)}, u32[]{:S(2)}) collective-permute-start(bf16[4,512,128]{2,1,0:T(8,128)(2,1)S(1)} %get-tuple-element.14.fitted), channel_id=1, source_target_pairs={{0,96},{16,112},{32,64},{48,80},{64,32},{80,48},{96,0},{112,16},{1... | collective-permute-start | bytes 1572872 | tf_op jit(solution)/shard_map/ppermute | solution.py:306
  56.9 0.8 copy-start.2
  60.7 14.0 %collective-permute-start.3 = (bf16[4,512,128]{2,1,0:T(8,128)(2,1)S(1)}, bf16[4,512,128]{2,1,0:T(8,128)(2,1)S(1)}, u32[]{:S(2)}, u32[]{:S(2)}) collective-permute-start(bf16[4,512,128]{2,1,0:T(8,128)(2,1)S(1)} %collective-permute-done.1.rest_1_), channel_id=1, source_target_pairs={{0,16},{16,0},{32,48},{48,32},{64,80},{80,64},{96,112},{112,96},{1... | collective-permute-start | bytes 1572872 | tf_op jit(solution)/shard_map/ppermute | solution.py:306
  63.8 13.4 %collective-permute-start.4 = (bf16[4,512,128]{2,1,0:T(8,128)(2,1)S(1)}, bf16[4,512,128]{2,1,0:T(8,128)(2,1)S(1)}, u32[]{:S(2)}, u32[]{:S(2)}) collective-permute-start(bf16[4,512,128]{2,1,0:T(8,128)(2,1)S(1)} %collective-permute-done.2.rest_2_), channel_id=1, source_target_pairs={{0,32},{16,48},{32,0},{48,16},{64,96},{80,112},{96,64},{112,80},{1... | collective-permute-start | bytes 1572872 | tf_op jit(solution)/shard_map/ppermute | solution.py:306
  64.6 14.9 %collective-permute-start.5 = (bf16[4,512,128]{2,1,0:T(8,128)(2,1)S(1)}, bf16[4,512,128]{2,1,0:T(8,128)(2,1)S(1)}, u32[]{:S(2)}, u32[]{:S(2)}) collective-permute-start(bf16[4,512,128]{2,1,0:T(8,128)(2,1)S(1)} %collective-permute-done.rest_0_), channel_id=1, source_target_pairs={{0,96},{16,112},{32,64},{48,80},{64,32},{80,48},{96,0},{112,16},{1... | collective-permute-start | bytes 1572872 | tf_op jit(solution)/shard_map/ppermute | solution.py:306
  75.4 47.6 %collective-permute-start.8 = (bf16[2,512,128]{2,1,0:T(8,128)(2,1)}, bf16[2,512,128]{2,1,0:T(8,128)(2,1)S(1)}, u32[]{:S(2)}, u32[]{:S(2)}) collective-permute-start(bf16[2,512,128]{2,1,0:T(8,128)(2,1)} %slice.64), channel_id=1, source_target_pairs={{0,96},{16,112},{32,64},{48,80},{64,32},{80,48},{96,0},{112,16},{1... | collective-permute-start | bytes 786440 | tf_op jit(solution)/shard_map/ppermute | solution.py:306
  77.8 45.2 %collective-permute-start.6 = (bf16[1,512,128]{2,1,0:T(8,128)(2,1)}, bf16[1,512,128]{2,1,0:T(8,128)(2,1)S(1)}, u32[]{:S(2)}, u32[]{:S(2)}) collective-permute-start(bf16[1,512,128]{2,1,0:T(8,128)(2,1)} %slice.62), channel_id=1, source_target_pairs={{0,16},{16,0},{32,48},{48,32},{64,80},{80,64},{96,112},{112,96},{1... | collective-permute-start | bytes 393224 | tf_op jit(solution)/shard_map/ppermute | solution.py:306
  80.2 42.8 %collective-permute-start.7 = (bf16[1,512,128]{2,1,0:T(8,128)(2,1)}, bf16[1,512,128]{2,1,0:T(8,128)(2,1)}, u32[]{:S(2)}, u32[]{:S(2)}) collective-permute-start(bf16[1,512,128]{2,1,0:T(8,128)(2,1)} %slice.63), channel_id=1, source_target_pairs={{0,32},{16,48},{32,0},{48,16},{64,96},{80,112},{96,64},{112,80},{1... | collective-permute-start | bytes 393224 | tf_op jit(solution)/shard_map/ppermute | solution.py:306
  95.6 1.0 copy-start.3
  96.6 1.0 copy-start.5
  97.7 0.7 copy-start.7
  98.4 0.6 copy-start.12
  99.0 0.7 copy-start.14
  99.7 0.7 copy-start.18
  107.1 1.3 copy-start
  108.4 2.2 %copy-start.8 = (f32[5,16,128]{2,1,0:T(8,128)}, f32[5,16,128]{2,1,0:T(8,128)S(1)}, u32[]{:S(2)}) copy-start(f32[5,16,128]{2,1,0:T(8,128)S(1)} %get-tuple-element.20) | copy-start | bytes 122884
  108.4 0.7 copy-start.6
  109.1 0.7 copy-start.15
  109.8 0.8 copy-start.16
  110.6 12.4 %copy-start.10 = (f32[5,16,128]{2,1,0:T(8,128)}, f32[5,16,128]{2,1,0:T(8,128)S(1)}, u32[]{:S(2)}) copy-start(f32[5,16,128]{2,1,0:T(8,128)S(1)} %get-tuple-element.21) | copy-start | bytes 122884
  110.7 12.4 %copy-start.13 = (f32[80]{0:T(128)S(1)}, f32[80]{0:T(128)}, u32[]{:S(2)}) copy-start(f32[80]{0:T(128)} %reshape.104.screen) | copy-start | bytes 964
  136.9 15.2 %copy-start.9 = (f32[5,16,128]{2,1,0:T(8,128)S(1)}, f32[5,16,128]{2,1,0:T(8,128)}, u32[]{:S(2)}) copy-start(f32[5,16,128]{2,1,0:T(8,128)} %copy-done.8) | copy-start | bytes 122884
  136.9 15.2 %copy-start.11 = (f32[5,16,128]{2,1,0:T(8,128)S(1)}, f32[5,16,128]{2,1,0:T(8,128)}, u32[]{:S(2)}) copy-start(f32[5,16,128]{2,1,0:T(8,128)} %copy-done.10) | copy-start | bytes 122884
  136.9 43.8 %all-to-all-start.1 = ((bf16[16,4,128,128]{3,2,1,0:T(8,128)(2,1)}), bf16[16,4,128,128]{3,2,1,0:T(8,128)(2,1)}, u32[]{:S(2)}, u32[]{:S(2)}) async-start(bf16[16,4,128,128]{3,2,1,0:T(8,128)(2,1)} %get-tuple-element.19), calls=%async_computation.1 | async-start | bytes 4194304 | tf_op jit(solution)/shard_map/all_to_all | solution.py:361
